TPU v7x, 32 devices: a whole 2x2x4 slice. The times are simulated.
32 devices in a mesh: seq: 4 (over y, x), dp: 2 (over core), mp: 4 (over z).
Axes of the slice: x: 2, y: 2, z: 4, core: 2. Of those that a mesh axis runs over, the one named last changes fastest.
Arguments:
- tokens: bfloat16 [8, 2048, 2048], P('dp', 'seq', 'mp'), may hold values from -6 to 6
- cotangent: bfloat16 [8, 2048, 2048], P('dp', 'seq', 'mp'), may hold values from -6 to 6
- domain_id: int32 [8], P('dp'), may hold values from 0 to 7
- domain_weight: int32 [8], replicated, may hold values from 1 to 4
- lower_level: int32 [2048], P('mp'), may hold values from 2 to 23
- norm_in: float32 [2048], P('mp'), may hold values from 0.1 to 1.9
- w_input: bfloat16 [2048, 2048], P(None, 'mp'), may hold values from -0.125 to 0.125
- w_forget: bfloat16 [2048, 2048], P(None, 'mp'), may hold values from -0.125 to 0.125
- w_gate_out: bfloat16 [2048, 2048], P(None, 'mp'), may hold values from -0.125 to 0.125
- out_gain: float32 [2048], P('mp'), may hold values from 0.1 to 1.9
- w_out: bfloat16 [2048, 2048], P('mp'), may hold values from -0.125 to 0.125
- norm_mid: float32 [2048], P('mp'), may hold values from 0.1 to 1.9
- w_gate: bfloat16 [2048, 5632], P(None, 'mp'), may hold values from -0.125 to 0.125
- w_up: bfloat16 [2048, 5632], P(None, 'mp'), may hold values from -0.125 to 0.125
- w_down: bfloat16 [5632, 2048], P('mp'), may hold values from -0.078125 to 0.078125
Outputs:
- mixed: bfloat16 [8, 2048, 2048], P('dp', 'seq', 'mp')
- grad_tokens: float32 [8, 2048, 2048], P('dp', 'seq', 'mp')
- grad_norm_in: float32 [2048], P('mp')
- grad_w_input: float32 [2048, 2048], P(None, 'mp')
- grad_w_forget: float32 [2048, 2048], P(None, 'mp')
- grad_w_gate_out: float32 [2048, 2048], P(None, 'mp')
- grad_out_gain: float32 [2048], P('mp')
- grad_w_out: float32 [2048, 2048], P('mp')
- grad_norm_mid: float32 [2048], P('mp')
- grad_w_gate: float32 [2048, 5632], P(None, 'mp')
- grad_w_up: float32 [2048, 5632], P(None, 'mp')
- grad_w_down: float32 [5632, 2048], P('mp')
All inputs are finite; a program needn't handle non-finite values.
Results may differ from a plain program's by a relative error of at most 0.0075.
The roundings to bfloat16 on the way count: a program that leaves them out, or rounds other values in their place, can miss the bound.
Values may be sent and summed in bfloat16 or wider, within the bound.
No kernel may reach another device: no remote copies, remote signals or barrier semaphores. Data moves between devices by JAX's collectives and lax.ppermute only.
A program may use at most 320 MiB of HBM per device.

v0:
```python
import jax
import jax.numpy as jnp
from jax import lax
from jax.sharding import PartitionSpec as P

EPS = 1e-06


def entering(value, axis, join, neutral, backward):
    count, mine = (lax.axis_size(axis), lax.axis_index(axis))
    pieces = jax.tree.map(lambda part: lax.all_gather(part, axis), value)
    if backward:
        pieces = jax.tree.map(lambda part: part[::-1], pieces)
        mine = count - 1 - mine
    so_far = jax.tree.map(
        lambda part, zero: jnp.full_like(part, 0) + jnp.asarray(zero, part.dtype), value, neutral
    )

    def lap(position, so_far):
        longer = join(so_far, jax.tree.map(lambda part: part[position], pieces))
        return jax.tree.map(lambda new, old: jnp.where(position < mine, new, old), longer, so_far)

    return lax.fori_loop(0, count - 1, lap, so_far)


def row_total(values):
    return lax.psum(values, "mp")


def chain_pairs(earlier, later):
    return (earlier[0] * later[0], later[0] * earlier[1] + later[1])


def swish_slope(values):
    sigma = jax.nn.sigmoid(values)
    return sigma * (1.0 + values * (1.0 - sigma))


def contract_rows(left, right):
    return lax.dot_general(
        left, right, (((0,), (0,)), ((), ())), preferred_element_type=jnp.float32
    )


def contract_last(left, right):
    return lax.dot_general(
        left, right, (((1,), (1,)), ((), ())), preferred_element_type=jnp.float32
    )


def per_device(
    tokens,
    cotangent,
    domain_id,
    domain_weight,
    lower_level,
    norm_in,
    w_input,
    w_forget,
    w_gate_out,
    out_gain,
    w_out,
    norm_mid,
    w_gate,
    w_up,
    w_down,
):
    seq_count, block_len, own_width = tokens.shape
    row_count = seq_count * block_len
    full_width = own_width * lax.axis_size("mp")
    ff_local = w_gate.shape[1]
    x_rows = tokens.astype(jnp.float32).reshape(row_count, own_width)
    scale_in = lax.rsqrt(row_total(jnp.sum(x_rows * x_rows, 1)) / full_width + EPS)[:, None]
    x_hat = x_rows * scale_in
    normed_full = lax.all_gather((x_hat * norm_in).astype(jnp.bfloat16), "mp", axis=1, tiled=True)
    w_mix = jnp.concatenate((w_input, w_forget, w_gate_out), 1)
    projected = jnp.dot(normed_full, w_mix, preferred_element_type=jnp.float32)
    in_raw = projected[:, :own_width]
    forget_raw = projected[:, own_width : 2 * own_width]
    gate_raw = projected[:, 2 * own_width :]
    lower = 1.0 - jnp.exp2(-0.5 * lower_level.astype(jnp.float32))
    forget_sig = jax.nn.sigmoid(forget_raw)
    forget = lower + (1.0 - lower) * forget_sig
    in_act = jax.nn.silu(in_raw)
    inflow = in_act * (1.0 - forget)
    forget_seq = forget.reshape(seq_count, block_len, own_width)
    decay_run, state_run = lax.associative_scan(
        chain_pairs, (forget_seq, inflow.reshape(seq_count, block_len, own_width)), axis=1
    )
    unit_decay = jnp.ones((seq_count, own_width), jnp.float32)
    zero_state = jnp.zeros((seq_count, own_width), jnp.float32)
    carried_in = entering(
        (decay_run[:, -1], state_run[:, -1]), "seq", chain_pairs, (unit_decay, zero_state), False
    )
    state_in = carried_in[1]
    state_seq = state_run + decay_run * state_in[:, None, :]
    state = state_seq.reshape(row_count, own_width)
    scale_state = lax.rsqrt(row_total(jnp.sum(state * state, 1)) / full_width + EPS)[:, None]
    state_hat = state * scale_state
    gate_act = jax.nn.silu(gate_raw)
    gated = (state_hat * out_gain * gate_act).astype(jnp.bfloat16)
    out_cols = lax.all_to_all(w_out, "mp", split_axis=1, concat_axis=0, tiled=True)
    gated_full = lax.all_gather(gated, "mp", axis=1, tiled=True)
    branch = jnp.dot(gated_full, out_cols, preferred_element_type=jnp.float32)
    resid = x_rows + branch
    scale_mid = lax.rsqrt(row_total(jnp.sum(resid * resid, 1)) / full_width + EPS)[:, None]
    resid_hat = resid * scale_mid
    second_full = lax.all_gather(
        (resid_hat * norm_mid).astype(jnp.bfloat16), "mp", axis=1, tiled=True
    )
    w_pair = jnp.concatenate((w_gate, w_up), 1)

    def glu_inner(source):
        both = jnp.dot(source, w_pair, preferred_element_type=jnp.float32)
        return (both[:, :ff_local], both[:, ff_local:])

    gate_value, up_value = glu_inner(second_full)
    hidden_act = (jax.nn.silu(gate_value) * up_value).astype(jnp.bfloat16)
    glu_term = lax.psum_scatter(
        jnp.dot(hidden_act, w_down, preferred_element_type=jnp.float32),
        "mp",
        scatter_dimension=1,
        tiled=True,
    )
    block_out = resid + glu_term
    mixed = block_out.astype(jnp.bfloat16).reshape(seq_count, block_len, own_width)
    domain_hits = domain_id[:, None] == jnp.arange(domain_weight.shape[0], dtype=jnp.int32)[None, :]
    seq_weight = jnp.sum(jnp.where(domain_hits, domain_weight[None, :], 0), 1).astype(jnp.float32)
    grad_out = (cotangent.astype(jnp.float32) * seq_weight[:, None, None]).reshape(
        row_count, own_width
    )
    grad_out_full = lax.all_gather(grad_out.astype(jnp.bfloat16), "mp", axis=1, tiled=True)
    grad_hidden = contract_last(grad_out_full, w_down)
    grad_w_down = contract_rows(hidden_act, grad_out_full)
    gate_back, up_back = glu_inner(lax.optimization_barrier(second_full))
    gate_sigma = jax.nn.sigmoid(gate_back)
    grad_gate = (
        grad_hidden * up_back * gate_sigma * (1.0 + gate_back * (1.0 - gate_sigma))
    ).astype(jnp.bfloat16)
    grad_up = (grad_hidden * gate_back * gate_sigma).astype(jnp.bfloat16)
    grad_pair = jnp.concatenate((grad_gate, grad_up), 1)
    grad_w_pair = contract_rows(second_full, grad_pair)
    grad_second = lax.psum_scatter(
        contract_last(grad_pair, w_pair), "mp", scatter_dimension=1, tiled=True
    )
    grad_norm_mid = jnp.sum(grad_second * resid_hat, 0)
    grad_mid_hat = grad_second * norm_mid
    mid_dot = row_total(jnp.sum(grad_mid_hat * resid_hat, 1))[:, None] / full_width
    grad_resid = grad_out + scale_mid * (grad_mid_hat - resid_hat * mid_dot)
    grad_resid_full = lax.all_gather(grad_resid.astype(jnp.bfloat16), "mp", axis=1, tiled=True)
    grad_w_out = contract_rows(gated, grad_resid_full)
    grad_gated = contract_last(grad_resid_full, w_out)
    grad_out_gain = jnp.sum(grad_gated * state_hat * gate_act, 0)
    grad_gate_raw = (grad_gated * state_hat * out_gain * swish_slope(gate_raw)).astype(jnp.bfloat16)
    grad_state_hat = grad_gated * out_gain * gate_act
    state_dot = row_total(jnp.sum(grad_state_hat * state_hat, 1))[:, None] / full_width
    grad_state = scale_state * (grad_state_hat - state_hat * state_dot)
    grad_state_seq = grad_state.reshape(seq_count, block_len, own_width)
    back_decay, back_run = lax.associative_scan(
        chain_pairs, (forget_seq, forget_seq * grad_state_seq), reverse=True, axis=1
    )
    carried_back = entering(
        (back_decay[:, 0], back_run[:, 0]), "seq", chain_pairs, (unit_decay, zero_state), True
    )
    later_in = carried_back[1]
    passed = back_run + back_decay * later_in[:, None, :]
    adjoint_seq = grad_state_seq + jnp.concatenate((passed[:, 1:], later_in[:, None, :]), 1)
    prev_state = jnp.concatenate((state_in[:, None, :], state_seq[:, :-1]), 1)
    adjoint = adjoint_seq.reshape(row_count, own_width)
    prev_rows = prev_state.reshape(row_count, own_width)
    grad_forget = adjoint * prev_rows - adjoint * in_act
    grad_in_raw = (adjoint * (1.0 - forget) * swish_slope(in_raw)).astype(jnp.bfloat16)
    grad_forget_raw = (grad_forget * (1.0 - lower) * forget_sig * (1.0 - forget_sig)).astype(
        jnp.bfloat16
    )
    grad_projected = jnp.concatenate((grad_in_raw, grad_forget_raw, grad_gate_raw), 1)
    grad_w_mix = contract_rows(normed_full, grad_projected)
    grad_normed = lax.psum_scatter(
        contract_last(grad_projected, w_mix), "mp", scatter_dimension=1, tiled=True
    )
    grad_norm_in = jnp.sum(grad_normed * x_hat, 0)
    grad_in_hat = grad_normed * norm_in
    in_dot = row_total(jnp.sum(grad_in_hat * x_hat, 1))[:, None] / full_width
    grad_tokens = grad_resid + scale_in * (grad_in_hat - x_hat * in_dot)
    totals = lax.psum(
        (
            grad_norm_in,
            grad_w_mix[:, :own_width],
            grad_w_mix[:, own_width : 2 * own_width],
            grad_w_mix[:, 2 * own_width :],
            grad_out_gain,
            grad_w_out,
            grad_norm_mid,
            grad_w_pair[:, :ff_local],
            grad_w_pair[:, ff_local:],
            grad_w_down,
        ),
        ("seq", "dp"),
    )
    return (
        mixed,
        grad_tokens.reshape(seq_count, block_len, own_width),
        totals[0],
        totals[1],
        totals[2],
        totals[3],
        totals[4],
        totals[5],
        totals[6],
        totals[7],
        totals[8],
        totals[9],
    )


def solution(mesh):
    in_specs = (
        P("dp", "seq", "mp"),
        P("dp", "seq", "mp"),
        P("dp"),
        P(),
        P("mp"),
        P("mp"),
        P(None, "mp"),
        P(None, "mp"),
        P(None, "mp"),
        P("mp"),
        P("mp", None),
        P("mp"),
        P(None, "mp"),
        P(None, "mp"),
        P("mp", None),
    )
    out_specs = (
        P("dp", "seq", "mp"),
        P("dp", "seq", "mp"),
        P("mp"),
        P(None, "mp"),
        P(None, "mp"),
        P(None, "mp"),
        P("mp"),
        P("mp", None),
        P("mp"),
        P(None, "mp"),
        P(None, "mp"),
        P("mp", None),
    )
    return jax.shard_map(
        per_device, mesh=mesh, in_specs=in_specs, out_specs=out_specs, check_vma=False
    )
```

profile of v0, /device:TPU:0, one launch (start us, length us, event | category | flops | bytes accessed | tf_op | source)
XLA Modules:
  0.0 3189.1 jit_solution(3619002101023223962)
XLA Ops:
  32.6 142.7 %all-gather.10.cloned.1.call-done = bf16[2048,2048]{1,0:T(8,128)(2,1)} async-done(((bf16[2048,512]{1,0:T(8,128)(2,1)}), bf16[2048,2048]{1,0:T(8,128)(2,1)}) %all-gather.10.cloned.1.call-update) | async-done | bytes 8388624 | tf_op jit(solution)/shard_map/all_gather | solution.py:75
  175.3 17.4 fusion.66
  525.9 103.7 %all_to_all.19 = bf16[512,4,512]{0,2,1:T(8,128)(2,1)} all-to-all(bf16[512,4,512]{0,2,1:T(8,128)(2,1)} %bitcast.155), channel_id=1, replica_groups=mesh['seq'=4,'dp'=2,'mp'=4] {'mp'}, dimensions={1} | all-to-all | bytes 4194304 | tf_op jit(solution)/shard_map/all_to_all | solution.py:102
  633.7 74.8 %all-gather.12.cloned.1.call-done = bf16[2048,2048]{1,0:T(8,128)(2,1)} async-done(((bf16[2048,512]{1,0:T(8,128)(2,1)}), bf16[2048,2048]{1,0:T(8,128)(2,1)}) %all-gather.12.cloned.1.call-update) | async-done | bytes 8388624 | tf_op jit(solution)/shard_map/all_gather | solution.py:103
  750.5 130.5 %all-gather.14.cloned.1.call-done = bf16[2048,2048]{1,0:T(8,128)(2,1)} async-done(((bf16[2048,512]{1,0:T(8,128)(2,1)}), bf16[2048,2048]{1,0:T(8,128)(2,1)}) %all-gather.14.cloned.1.call-update) | async-done | bytes 8388624 | tf_op jit(solution)/shard_map/all_gather | solution.py:108
  881.0 32.1 %fusion.69 = f32[2048,2816]{1,0:T(8,128)} fusion(bf16[2048,2048]{1,0:T(8,128)(2,1)} %all-gather.14.cloned.1.call-done, bf16[2048,2816]{1,0:T(8,128)(2,1)} %constant_dynamic-update-slice_fusion.3), kind=kOutput, calls=%fused_computation.224 | convolution fusion | flops 23622320128 | bytes 42991616 | tf_op jit(solution)/shard_map/dot_general | solution.py:114
  913.1 117.8 %all-gather.16.cloned.1.call-done = bf16[2048,2048]{1,0:T(8,128)(2,1)} async-done(((bf16[2048,512]{1,0:T(8,128)(2,1)}), bf16[2048,2048]{1,0:T(8,128)(2,1)}) %all-gather.16.cloned.1.call-update) | async-done | bytes 8388624 | tf_op jit(solution)/shard_map/all_gather | solution.py:132
  1030.8 24.2 fusion.4
  1055.0 32.2 %fusion.7 = f32[2048,2048]{1,0:T(8,128)} fusion(bf16[2048,2816]{1,0:T(8,128)(2,1)} %constant_dynamic-update-slice_fusion.3, bf16[2048,1408]{1,0:T(8,128)(2,1)} %get-tuple-element.281, bf16[2048,1408]{1,0:T(8,128)(2,1)} %get-tuple-element.280), kind=kOutput, calls=%fused_computation.16 | convolution fusion | flops 23645388800 | bytes 39845888 | tf_op jit(solution)/shard_map/dot_general | solution.py:46
  1087.3 30.6 fusion.67
  1124.0 19.2 fusion.68
  1143.2 222.7 %reduce-scatter.6.cloned.1.call-done = f32[2048,512]{1,0:T(8,128)} async-done(((f32[2048,2048]{1,0:T(8,128)}), f32[2048,512]{1,0:T(8,128)}) %reduce-scatter.6.cloned.1.call-update) | async-done | bytes 4194320 | tf_op jit(solution)/shard_map/reduce_scatter | solution.py:143
  1382.2 267.3 %reduce-scatter.4.cloned.1.call-done = f32[2048,512]{1,0:T(8,128)} async-done(((f32[2048,2048]{1,0:T(8,128)}), f32[2048,512]{1,0:T(8,128)}) %reduce-scatter.4.cloned.1.call-update) | async-done | bytes 4194320 | tf_op jit(solution)/shard_map/reduce_scatter | solution.py:119
  1713.4 96.8 %all-gather.18.cloned.1.call-done = bf16[2048,2048]{1,0:T(8,128)(2,1)} async-done(((bf16[2048,512]{1,0:T(8,128)(2,1)}), bf16[2048,2048]{1,0:T(8,128)(2,1)}) %all-gather.18.cloned.1.call-update) | async-done | bytes 8388624 | tf_op jit(solution)/shard_map/all_gather | solution.py:150
  2056.5 17.1 slice.755
  2155.9 32.5 %rev.14 = f32[4,512,512]{2,1,0:T(8,128)} reverse(f32[4,512,512]{2,1,0:T(8,128)} %add.592), dimensions={1} | reverse | bytes 8388608 | tf_op jit(solution)/shard_map/rev | solution.py:159
  2188.4 32.5 %rev.15 = f32[4,512,512]{2,1,0:T(8,128)} reverse(f32[4,512,512]{2,1,0:T(8,128)} %add.601), dimensions={1} | reverse | bytes 8388608 | tf_op jit(solution)/shard_map/rev | solution.py:159
  2237.2 18.9 fusion.31
  2256.1 33.2 %fusion.6 = f32[2048,2816]{1,0:T(8,128)} fusion(bf16[2048,2048]{1,0:T(8,128)(2,1)} %all-gather.14.cloned.1.call-done, bf16[2048,1408]{1,0:T(8,128)(2,1)} %get-tuple-element.281, bf16[2048,1408]{1,0:T(8,128)(2,1)} %get-tuple-element.280), kind=kOutput, calls=%fused_computation.15 | convolution fusion | flops 23645388800 | bytes 42991616 | tf_op jit(solution)/shard_map/dot_general | solution.py:40
  2289.4 17.2 fusion.59
  2306.6 19.2 fusion.71
  2325.8 17.0 fusion.30
  2362.5 172.1 %reduce-scatter.8.cloned.1.call-done = f32[2048,512]{1,0:T(8,128)} async-done(((f32[2048,2048]{1,0:T(8,128)}), f32[2048,512]{1,0:T(8,128)}) %reduce-scatter.8.cloned.1.call-update) | async-done | bytes 4194320 | tf_op jit(solution)/shard_map/reduce_scatter | solution.py:178
  2569.4 568.9 %all-reduce.76.cloned.1.call-done = (f32[2048,512]{1,0:T(8,128)}, f32[2048,512]{1,0:T(8,128)}, f32[2048,512]{1,0:T(8,128)}, f32[512,2048]{1,0:T(8,128)}, f32[204...) async-done(((f32[2048,512]{1,0:T(8,128)}, f32[2048,512]{1,0:T(8,128)}, f32[2048,512]{1,0:T(8,128)}, f32[512,2048]{1,0:T(8,128)}, f32[2048,1408]{1,0:T(8,128)}, ...) | async-done | bytes 51380240 | tf_op jit(solution)/shard_map/psum | solution.py:185
  (618 shorter events, 932.4 us)
Async XLA Ops:
  7.2 168.1 %all-gather.10.cloned.1.call-start = ((), (), s32[]{:S(2)}) async-start(), calls=%async_computation.4 | async-start | bytes 10485760 | tf_op jit(solution)/shard_map/all_gather | solution.py:75
  27.3 681.2 %all-gather.12.cloned.1.call-start = ((), (), s32[]{:S(2)}) async-start(), calls=%async_computation.5 | async-start | bytes 10485760 | tf_op jit(solution)/shard_map/all_gather | solution.py:103
  27.4 165.3 %copy-start.104 = (f32[512]{0:T(512)}, f32[512]{0:T(512)S(1)}, u32[]{:S(2)}) copy-start(f32[512]{0:T(512)S(1)} %get-tuple-element.371) | copy-start | bytes 6148
  251.4 29.6 copy-start.17
  372.6 27.7 copy-start.53
  523.3 357.7 %all-gather.14.cloned.1.call-start = ((), (), s32[]{:S(2)}) async-start(), calls=%async_computation.6 | async-start | bytes 10485760 | tf_op jit(solution)/shard_map/all_gather | solution.py:108
  525.9 182.6 %copy-start.6 = (bf16[4,512,512]{2,1,0:T(8,128)(2,1)S(1)}, bf16[4,512,512]{2,1,0:T(8,128)(2,1)}, u32[]{:S(2)}) copy-start(bf16[4,512,512]{2,1,0:T(8,128)(2,1)} %param.19) | copy-start | bytes 6291460
  733.9 296.9 %all-gather.16.cloned.1.call-start = ((), (), s32[]{:S(2)}) async-start(), calls=%async_computation.8 | async-start | bytes 10485760 | tf_op jit(solution)/shard_map/all_gather | solution.py:132
  738.5 627.4 %reduce-scatter.6.cloned.1.call-start = ((), (), s32[]{:S(2)}) async-start(), calls=%async_computation.9 | async-start | bytes 20971520 | tf_op jit(solution)/shard_map/reduce_scatter | solution.py:143
  1087.2 562.2 %reduce-scatter.4.cloned.1.call-start = ((), (), s32[]{:S(2)}) async-start(), calls=%async_computation.7 | async-start | bytes 20971520 | tf_op jit(solution)/shard_map/reduce_scatter | solution.py:119
  1143.1 222.7 %copy-start.64 = (f32[2048]{0:T(1024)S(1)}, f32[2048]{0:T(1024)}, u32[]{:S(2)}) copy-start(f32[2048]{0:T(1024)} %copy-done.63) | copy-start | bytes 24580
  1143.1 222.7 %copy-start.103 = (f32[512]{0:T(512)S(1)}, f32[512]{0:T(512)}, u32[]{:S(2)}) copy-start(f32[512]{0:T(512)} %param.30) | copy-start | bytes 6148
  1143.2 667.0 %all-gather.18.cloned.1.call-start = ((), (), s32[]{:S(2)}) async-start(), calls=%async_computation.10 | async-start | bytes 10485760 | tf_op jit(solution)/shard_map/all_gather | solution.py:150
  1659.5 875.2 %reduce-scatter.8.cloned.1.call-start = ((), (), s32[]{:S(2)}) async-start(), calls=%async_computation.11 | async-start | bytes 20971520 | tf_op jit(solution)/shard_map/reduce_scatter | solution.py:178
  1708.3 101.9 %copy-start.39 = (bf16[512,2048]{1,0:T(8,128)(2,1)S(1)}, bf16[512,2048]{1,0:T(8,128)(2,1)}, u32[]{:S(2)}) copy-start(bf16[512,2048]{1,0:T(8,128)(2,1)} %param.29) | copy-start | bytes 6291460
  1708.3 101.9 %copy-start.66 = (f32[2048]{0:T(1024)S(1)}, f32[2048]{0:T(1024)}, u32[]{:S(2)}) copy-start(f32[2048]{0:T(1024)} %copy-done.65) | copy-start | bytes 24580
  1708.3 101.9 %copy-start.107 = (f32[512]{0:T(512)S(1)}, f32[512]{0:T(512)}, u32[]{:S(2)}) copy-start(f32[512]{0:T(512)} %param.28) | copy-start | bytes 6148
  2256.1 882.2 %all-reduce.76.cloned.1.call-start = ((), (), s32[]{:S(2)}) async-start(), calls=%async_computation.12 | async-start | bytes 102760448 | tf_op jit(solution)/shard_map/psum | solution.py:185
  2289.4 36.4 %slice-start = ((s8[8388608]{0:T(1024)(128)(4,1)}), s8[4194304]{0:T(1024)(128)(4,1)S(1)}, s32[]{:S(2)}) async-start(s8[8388608]{0:T(1024)(128)(4,1)} %bitcast.195), calls=%async_computation.13 | async-start | bytes 8388608
  2362.5 172.2 %copy-start.7 = (bf16[4,512,512]{2,1,0:T(8,128)(2,1)S(1)}, bf16[4,512,512]{2,1,0:T(8,128)(2,1)}, u32[]{:S(2)}) copy-start(bf16[4,512,512]{2,1,0:T(8,128)(2,1)} %param.19) | copy-start | bytes 6291460
  2362.5 172.2 %copy-start.58 = (f32[2048]{0:T(1024)S(1)}, f32[2048]{0:T(1024)}, u32[]{:S(2)}) copy-start(f32[2048]{0:T(1024)} %copy-done.57) | copy-start | bytes 24580
  2362.5 172.2 %copy-start.101 = (f32[512]{0:T(512)S(1)}, f32[512]{0:T(512)}, u32[]{:S(2)}) copy-start(f32[512]{0:T(512)} %param.24) | copy-start | bytes 6148
  2362.5 175.1 %copy-start.108 = (f32[512]{0:T(512)S(1)}, f32[512]{0:T(512)}, u32[]{:S(2)}) copy-start(f32[512]{0:T(512)} %get-tuple-element.240) | copy-start | bytes 6148
  2362.5 175.1 %copy-start.110 = (f32[512]{0:T(512)S(1)}, f32[512]{0:T(512)}, u32[]{:S(2)}) copy-start(f32[512]{0:T(512)} %get-tuple-element.238) | copy-start | bytes 6148
  (100 other events, 1155.3 us)
Sparse Core Ops, SparseCore 0:
  27.4 147.8 all-gather.9
  523.4 185.0 all-gather.11
  734.1 146.8 all-gather.13
  883.0 147.8 all-gather.15
  1087.4 278.4 reduce-scatter.5
  1368.2 281.2 reduce-scatter.3
  1659.6 150.5 all-gather.17
  2256.2 278.4 reduce-scatter.7
  2541.7 596.4 all-reduce.75
where the time goes:
time: 3220 us; the launch traced here: 3190 us
  waiting for transfers between devices  1790 us (56%)
  local copies, waits for them, and re-layouts  679 us (21%)
  matrix products  278 us (9%)
  blocking collectives  216 us (7%)
  other arithmetic  206 us (6%)
    psum x1, waiting for transfers between devices, per_device(): lax.psum((grad_norm_in, grad_w_mix[:, :own_width], grad_w_mix[:, own_widt...  569 us
    reduce_scatter x1, waiting for transfers between devices, per_device(): lax.psum_scatter(jnp.dot(hidden_act, w_down, preferred_element_type=jnp.f...  267 us
    slice x64, local copies, waits for them, and re-layouts, per_device(): lax.associative_scan(chain_pairs, (forget_seq, forget_seq * grad_state_se...  229 us
    reduce_scatter x1, waiting for transfers between devices, per_device(): lax.psum_scatter(contract_last(grad_pair, w_pair), 'mp', scatter_dimensio...  223 us
    slice x59, local copies, waits for them, and re-layouts, per_device(): lax.associative_scan(chain_pairs, (forget_seq, inflow.reshape(seq_count,...  176 us
    reduce_scatter x1, waiting for transfers between devices, per_device(): lax.psum_scatter(contract_last(grad_projected, w_mix), 'mp', scatter_dime...  172 us
    all_gather x1, waiting for transfers between devices, per_device(): lax.all_gather((x_hat * norm_in).astype(jnp.bfloat16), 'mp', axis=1, tile...  143 us
    all_gather x1, waiting for transfers between devices, per_device(): lax.all_gather((resid_hat * norm_mid).astype(jnp.bfloat16), 'mp', axis=1,...  130 us
  transfers between devices with their start and end apart: 9, of which 9 were waited for; matrix products, arithmetic and copies ran while one was open for 9% of the time, Pallas kernels for 0%

commit v1 on v0

--- a/solution.py
+++ b/solution.py
@@ -183,19 +183,22 @@
     in_dot = row_total(jnp.sum(grad_in_hat * x_hat, 1))[:, None] / full_width
     grad_tokens = grad_resid + scale_in * (grad_in_hat - x_hat * in_dot)
     totals = lax.psum(
-        (
-            grad_norm_in,
-            grad_w_mix[:, :own_width],
-            grad_w_mix[:, own_width : 2 * own_width],
-            grad_w_mix[:, 2 * own_width :],
-            grad_out_gain,
-            grad_w_out,
-            grad_norm_mid,
-            grad_w_pair[:, :ff_local],
-            grad_w_pair[:, ff_local:],
-            grad_w_down,
+        lax.psum(
+            (
+                grad_norm_in,
+                grad_w_mix[:, :own_width],
+                grad_w_mix[:, own_width : 2 * own_width],
+                grad_w_mix[:, 2 * own_width :],
+                grad_out_gain,
+                grad_w_out,
+                grad_norm_mid,
+                grad_w_pair[:, :ff_local],
+                grad_w_pair[:, ff_local:],
+                grad_w_down,
+            ),
+            "dp",
         ),
-        ("seq", "dp"),
+        "seq",
     )
     return (
         mixed,

time: 3220 us -> 3670 us (1.14)
  waiting for transfers between devices: 1790 us -> 2250 us
    psum x0 -> x1, waiting for transfers between devices: none -> 851 us  [per_device(): lax.psum(lax.psum((grad_norm_in, grad_w_mix[:, :own_width], grad_w_mix[:,...]
    psum x1, waiting for transfers between devices: 569 us -> 130 us  [per_device(): lax.psum((grad_norm_in, grad_w_mix[:, :own_width], grad_w_mix[:, own_widt...]
    reduce_scatter x1, waiting for transfers between devices: 172 us -> 284 us  [per_device(): lax.psum_scatter(contract_last(grad_projected, w_mix), 'mp', scatter_dime...]
    reduce_scatter x1, waiting for transfers between devices: 223 us -> 169 us  [per_device(): lax.psum_scatter(contract_last(grad_pair, w_pair), 'mp', scatter_dimensio...]
  transfers between devices with their start and end apart: 9 -> 10, of which waited for: 9 -> 10; matrix products, arithmetic and copies ran while one was open for 9% -> 7% of each run, Pallas kernels for 0% -> 0%
where the time goes in v1:
time: 3670 us; the launch traced here: 3640 us
  waiting for transfers between devices  2250 us (61%)
  local copies, waits for them, and re-layouts  679 us (19%)
  matrix products  279 us (8%)
  blocking collectives  214 us (6%)
  other arithmetic  206 us (6%)
    psum x1, waiting for transfers between devices, per_device(): lax.psum(lax.psum((grad_norm_in, grad_w_mix[:, :own_width], grad_w_mix[:,...  851 us
    reduce_scatter x1, waiting for transfers between devices, per_device(): lax.psum_scatter(contract_last(grad_projected, w_mix), 'mp', scatter_dime...  284 us
    reduce_scatter x1, waiting for transfers between devices, per_device(): lax.psum_scatter(jnp.dot(hidden_act, w_down, preferred_element_type=jnp.f...  267 us
    slice x64, local copies, waits for them, and re-layouts, per_device(): lax.associative_scan(chain_pairs, (forget_seq, forget_seq * grad_state_se...  229 us
    slice x59, local copies, waits for them, and re-layouts, per_device(): lax.associative_scan(chain_pairs, (forget_seq, inflow.reshape(seq_count,...  176 us
    reduce_scatter x1, waiting for transfers between devices, per_device(): lax.psum_scatter(contract_last(grad_pair, w_pair), 'mp', scatter_dimensio...  169 us
    all_gather x1, waiting for transfers between devices, per_device(): lax.all_gather((x_hat * norm_in).astype(jnp.bfloat16), 'mp', axis=1, tile...  143 us
    all_gather x1, waiting for transfers between devices, per_device(): lax.all_gather((resid_hat * norm_mid).astype(jnp.bfloat16), 'mp', axis=1,...  130 us
  transfers between devices with their start and end apart: 10, of which 10 were waited for; matrix products, arithmetic and copies ran while one was open for 7% of the time, Pallas kernels for 0%

profile of v1, /device:TPU:0, one launch (start us, length us, event | category | flops | bytes accessed | tf_op | source)
XLA Modules:
  0.0 3644.7 jit_solution(17940196739189735219)
XLA Ops:
  32.8 142.5 %all-gather.10.cloned.1.call-done = bf16[2048,2048]{1,0:T(8,128)(2,1)} async-done(((bf16[2048,512]{1,0:T(8,128)(2,1)}), bf16[2048,2048]{1,0:T(8,128)(2,1)}) %all-gather.10.cloned.1.call-update) | async-done | bytes 8388624 | tf_op jit(solution)/shard_map/all_gather | solution.py:75
  175.3 17.4 fusion.66
  525.9 103.7 %all_to_all.19 = bf16[512,4,512]{0,2,1:T(8,128)(2,1)} all-to-all(bf16[512,4,512]{0,2,1:T(8,128)(2,1)} %bitcast.155), channel_id=1, replica_groups=mesh['seq'=4,'dp'=2,'mp'=4] {'mp'}, dimensions={1} | all-to-all | bytes 4194304 | tf_op jit(solution)/shard_map/all_to_all | solution.py:102
  633.7 74.8 %all-gather.12.cloned.1.call-done = bf16[2048,2048]{1,0:T(8,128)(2,1)} async-done(((bf16[2048,512]{1,0:T(8,128)(2,1)}), bf16[2048,2048]{1,0:T(8,128)(2,1)}) %all-gather.12.cloned.1.call-update) | async-done | bytes 8388624 | tf_op jit(solution)/shard_map/all_gather | solution.py:103
  750.5 130.5 %all-gather.14.cloned.1.call-done = bf16[2048,2048]{1,0:T(8,128)(2,1)} async-done(((bf16[2048,512]{1,0:T(8,128)(2,1)}), bf16[2048,2048]{1,0:T(8,128)(2,1)}) %all-gather.14.cloned.1.call-update) | async-done | bytes 8388624 | tf_op jit(solution)/shard_map/all_gather | solution.py:108
  880.9 32.1 fusion.69
  913.0 117.8 %all-gather.16.cloned.1.call-done = bf16[2048,2048]{1,0:T(8,128)(2,1)} async-done(((bf16[2048,512]{1,0:T(8,128)(2,1)}), bf16[2048,2048]{1,0:T(8,128)(2,1)}) %all-gather.16.cloned.1.call-update) | async-done | bytes 8388624 | tf_op jit(solution)/shard_map/all_gather | solution.py:132
  1030.8 24.1 fusion.4
  1054.9 32.2 fusion.7
  1087.2 30.6 fusion.67
  1123.9 19.0 fusion.68
  1196.5 169.3 %reduce-scatter.6.cloned.1.call-done = f32[2048,512]{1,0:T(8,128)} async-done(((f32[2048,2048]{1,0:T(8,128)}), f32[2048,512]{1,0:T(8,128)}) %reduce-scatter.6.cloned.1.call-update) | async-done | bytes 4194320 | tf_op jit(solution)/shard_map/reduce_scatter | solution.py:143
  1382.1 267.3 %reduce-scatter.4.cloned.1.call-done = f32[2048,512]{1,0:T(8,128)} async-done(((f32[2048,2048]{1,0:T(8,128)}), f32[2048,512]{1,0:T(8,128)}) %reduce-scatter.4.cloned.1.call-update) | async-done | bytes 4194320 | tf_op jit(solution)/shard_map/reduce_scatter | solution.py:119
  1659.5 32.5 fusion.6
  1709.0 19.3 fusion.71
  1728.3 81.8 %all-gather.18.cloned.1.call-done = bf16[2048,2048]{1,0:T(8,128)(2,1)} async-done(((bf16[2048,512]{1,0:T(8,128)(2,1)}), bf16[2048,2048]{1,0:T(8,128)(2,1)}) %all-gather.18.cloned.1.call-update) | async-done | bytes 8388624 | tf_op jit(solution)/shard_map/all_gather | solution.py:150
  2055.7 17.1 slice.755
  2155.1 32.5 rev.14
  2187.6 32.6 rev.15
  2236.5 18.4 fusion.30
  2274.6 20.3 fusion.31
  2294.9 130.3 %all-reduce.81.cloned.1.call-done = (f32[2048,512]{1,0:T(8,128)}, f32[2048,512]{1,0:T(8,128)}, f32[2048,512]{1,0:T(8,128)}, f32[512,2048]{1,0:T(8,128)}, f32[204...) async-done(((f32[2048,512]{1,0:T(8,128)}, f32[2048,512]{1,0:T(8,128)}, f32[2048,512]{1,0:T(8,128)}, f32[512,2048]{1,0:T(8,128)}, f32[2048,1408]{1,0:T(8,128)}, ...) | async-done | bytes 51380240 | tf_op jit(solution)/shard_map/psum | solution.py:186
  2425.3 283.8 %reduce-scatter.8.cloned.1.call-done = f32[2048,512]{1,0:T(8,128)} async-done(((f32[2048,2048]{1,0:T(8,128)}), f32[2048,512]{1,0:T(8,128)}) %reduce-scatter.8.cloned.1.call-update) | async-done | bytes 4194320 | tf_op jit(solution)/shard_map/reduce_scatter | solution.py:178
  2742.4 851.2 %all-reduce.79.cloned.1.call-done = (f32[2048,512]{1,0:T(8,128)}, f32[2048,512]{1,0:T(8,128)}, f32[2048,512]{1,0:T(8,128)}, f32[512,2048]{1,0:T(8,128)}, f32[204...) async-done(((f32[2048,512]{1,0:T(8,128)}, f32[2048,512]{1,0:T(8,128)}, f32[2048,512]{1,0:T(8,128)}, f32[512,2048]{1,0:T(8,128)}, f32[2048,1408]{1,0:T(8,128)}, ...) | async-done | bytes 51380240 | tf_op jit(solution)/shard_map/psum | solution.py:185
  (615 shorter events, 947.2 us)
Async XLA Ops:
  7.2 168.1 %all-gather.10.cloned.1.call-start = ((), (), s32[]{:S(2)}) async-start(), calls=%async_computation.4 | async-start | bytes 10485760 | tf_op jit(solution)/shard_map/all_gather | solution.py:75
  27.3 681.2 %all-gather.12.cloned.1.call-start = ((), (), s32[]{:S(2)}) async-start(), calls=%async_computation.5 | async-start | bytes 10485760 | tf_op jit(solution)/shard_map/all_gather | solution.py:103
  27.4 165.3 %copy-start.103 = (f32[512]{0:T(512)}, f32[512]{0:T(512)S(1)}, u32[]{:S(2)}) copy-start(f32[512]{0:T(512)S(1)} %get-tuple-element.381) | copy-start | bytes 6148
  251.4 29.6 copy-start.17
  372.5 27.7 copy-start.52
  523.3 357.6 %all-gather.14.cloned.1.call-start = ((), (), s32[]{:S(2)}) async-start(), calls=%async_computation.6 | async-start | bytes 10485760 | tf_op jit(solution)/shard_map/all_gather | solution.py:108
  525.9 182.7 %copy-start.6 = (bf16[4,512,512]{2,1,0:T(8,128)(2,1)S(1)}, bf16[4,512,512]{2,1,0:T(8,128)(2,1)}, u32[]{:S(2)}) copy-start(bf16[4,512,512]{2,1,0:T(8,128)(2,1)} %param.19) | copy-start | bytes 6291460
  733.9 296.9 %all-gather.16.cloned.1.call-start = ((), (), s32[]{:S(2)}) async-start(), calls=%async_computation.8 | async-start | bytes 10485760 | tf_op jit(solution)/shard_map/all_gather | solution.py:132
  738.5 627.3 %reduce-scatter.6.cloned.1.call-start = ((), (), s32[]{:S(2)}) async-start(), calls=%async_computation.9 | async-start | bytes 20971520 | tf_op jit(solution)/shard_map/reduce_scatter | solution.py:143
  1087.1 562.2 %reduce-scatter.4.cloned.1.call-start = ((), (), s32[]{:S(2)}) async-start(), calls=%async_computation.7 | async-start | bytes 20971520 | tf_op jit(solution)/shard_map/reduce_scatter | solution.py:119
  1142.9 667.2 %all-gather.18.cloned.1.call-start = ((), (), s32[]{:S(2)}) async-start(), calls=%async_computation.10 | async-start | bytes 10485760 | tf_op jit(solution)/shard_map/all_gather | solution.py:150
  1191.5 174.3 %copy-start.63 = (f32[2048]{0:T(1024)S(1)}, f32[2048]{0:T(1024)}, u32[]{:S(2)}) copy-start(f32[2048]{0:T(1024)} %copy-done.62) | copy-start | bytes 24580
  1191.5 174.3 %copy-start.102 = (f32[512]{0:T(512)S(1)}, f32[512]{0:T(512)}, u32[]{:S(2)}) copy-start(f32[512]{0:T(512)} %param.30) | copy-start | bytes 6148
  1659.4 765.8 %all-reduce.81.cloned.1.call-start = ((), (), s32[]{:S(2)}) async-start(), calls=%async_computation.13 | async-start | bytes 102760448 | tf_op jit(solution)/shard_map/psum | solution.py:186
  1709.0 101.1 %copy-start.39 = (bf16[512,2048]{1,0:T(8,128)(2,1)S(1)}, bf16[512,2048]{1,0:T(8,128)(2,1)}, u32[]{:S(2)}) copy-start(bf16[512,2048]{1,0:T(8,128)(2,1)} %param.29) | copy-start | bytes 6291460
  1709.0 101.1 %copy-start.65 = (f32[2048]{0:T(1024)S(1)}, f32[2048]{0:T(1024)}, u32[]{:S(2)}) copy-start(f32[2048]{0:T(1024)} %copy-done.64) | copy-start | bytes 24580
  1709.0 101.1 %copy-start.106 = (f32[512]{0:T(512)S(1)}, f32[512]{0:T(512)}, u32[]{:S(2)}) copy-start(f32[512]{0:T(512)} %param.28) | copy-start | bytes 6148
  2274.5 434.5 %reduce-scatter.8.cloned.1.call-start = ((), (), s32[]{:S(2)}) async-start(), calls=%async_computation.11 | async-start | bytes 20971520 | tf_op jit(solution)/shard_map/reduce_scatter | solution.py:178
  2294.9 1298.7 %all-reduce.79.cloned.1.call-start = ((), (), s32[]{:S(2)}) async-start(), calls=%async_computation.12 | async-start | bytes 102760448 | tf_op jit(solution)/shard_map/psum | solution.py:185
  2425.2 283.9 %copy-start.7 = (bf16[4,512,512]{2,1,0:T(8,128)(2,1)S(1)}, bf16[4,512,512]{2,1,0:T(8,128)(2,1)}, u32[]{:S(2)}) copy-start(bf16[4,512,512]{2,1,0:T(8,128)(2,1)} %param.19) | copy-start | bytes 6291460
  2425.2 283.9 %copy-start.57 = (f32[2048]{0:T(1024)S(1)}, f32[2048]{0:T(1024)}, u32[]{:S(2)}) copy-start(f32[2048]{0:T(1024)} %copy-done.56) | copy-start | bytes 24580
  2425.3 283.9 %copy-start.100 = (f32[512]{0:T(512)S(1)}, f32[512]{0:T(512)}, u32[]{:S(2)}) copy-start(f32[512]{0:T(512)} %param.24) | copy-start | bytes 6148
  2425.3 286.8 %copy-start.107 = (f32[512]{0:T(512)S(1)}, f32[512]{0:T(512)}, u32[]{:S(2)}) copy-start(f32[512]{0:T(512)} %get-tuple-element.240) | copy-start | bytes 6148
  2425.3 286.8 %copy-start.109 = (f32[512]{0:T(512)S(1)}, f32[512]{0:T(512)}, u32[]{:S(2)}) copy-start(f32[512]{0:T(512)} %get-tuple-element.238) | copy-start | bytes 6148
  (98 other events, 1106.4 us)
Sparse Core Ops, SparseCore 0:
  27.4 147.8 all-gather.9
  523.4 185.0 all-gather.11
  734.0 146.8 all-gather.13
  882.9 147.8 all-gather.15
  1087.3 278.4 reduce-scatter.5
  1368.1 281.1 reduce-scatter.3
  1659.5 150.5 all-gather.17
  2274.7 150.5 all-reduce.80
  2427.6 281.4 reduce-scatter.7
  2714.4 879.1 all-reduce.78
